TPU v7x, 128 devices: a whole 4x4x4 slice. The times are simulated.
128 devices in a mesh: row: 16 (over x, z), col: 8 (over y, core).
Axes of the slice: x: 4, y: 4, z: 4, core: 2. Of those that a mesh axis runs over, the one named last changes fastest.
Arguments:
- block_values: bfloat16 [16, 8, 256, 128, 128], P('row', 'col')
- block_rows: int32 [16, 8, 256], P('row', 'col'), may hold values from -1 to 511, as said below
- block_cols: int32 [16, 8, 256], P('row', 'col'), may hold values from -1 to 511, as said below
- cost_vec: float32 [524288], P('col')
- demand: float32 [1048576], P('row')
- lower: float32 [524288], P('col'), may hold values from -1.5 to -0.2
- upper: float32 [524288], P('col'), may hold values from 0.2 to 1.5
- bound_kind: int32 [524288], P('col'), may hold values from 0 to 3
- primal_start: float32 [524288], P('col'), may hold values from -4 to 4
- dual_start: float32 [1048576], P('row'), may hold values from 0 to 1.5
Outputs:
- primal_out: float32 [524288], P('col')
- dual_out: float32 [1048576], P('row')
Inputs may be any that keep to these rules, and one draw needn't show every extreme that they name: A slot's block_rows and block_cols are both -1 exactly when the slot is empty; the live slots of a device come first, a device has at least 64 of them, and in every draw some device has all 256 slots live and some device has empty slots; every block row and every block column of the whole matrix is named by some live slot; a block place may be named by several slots. `block_cols`: as for block_rows.
All inputs are finite; a program needn't handle non-finite values.
Results may differ from a plain program's by a relative error of at most 0.0073.
Values sent between devices are 32-bit elements; how exact they have to be, the bound alone decides.
A program may use at most 64 MiB of HBM per device.

v0:
```python
import jax
import jax.numpy as jnp
from jax import lax
from jax.sharding import PartitionSpec as P

RUIZ_PASSES = 2
ITERS = 2


SMALL_EPS = 1e-06
STEP_SCALE = 0.3


def pick_tiles(vector, slot_ids, tile_count):
    tile_width = vector.shape[0] // tile_count
    padded = jnp.concatenate(
        [vector.reshape(tile_count, tile_width), jnp.zeros((1, tile_width), vector.dtype)], axis=0
    )
    return padded[slot_ids]


def tile_peaks(block_terms, slot_ids, tile_count):
    tile_width = block_terms.shape[1]
    return (
        jnp.zeros((tile_count + 1, tile_width), jnp.float32)
        .at[slot_ids]
        .max(block_terms)[:tile_count]
        .reshape(-1)
    )


def tile_sums(block_terms, slot_ids, tile_count):
    tile_width = block_terms.shape[1]
    return (
        jnp.zeros((tile_count + 1, tile_width), jnp.float32)
        .at[slot_ids]
        .add(block_terms)[:tile_count]
        .reshape(-1)
    )


def project_bounds(values, low_side, high_side, bound_types):
    lifted = jnp.where(
        (bound_types == 1) | (bound_types == 3), jnp.maximum(values, low_side), values
    )
    return jnp.where(
        (bound_types == 2) | (bound_types == 3), jnp.minimum(lifted, high_side), lifted
    )


def per_device(
    block_values,
    block_rows,
    block_cols,
    cost_vec,
    demand,
    lower,
    upper,
    bound_kind,
    primal_start,
    dual_start,
):
    values = block_values[0, 0]
    row_ids = block_rows[0, 0]
    col_ids = block_cols[0, 0]
    tile_width = values.shape[1]
    row_length = demand.shape[0]
    col_length = cost_vec.shape[0]
    row_count = row_length // tile_width
    col_count = col_length // tile_width
    live_slot = row_ids >= 0
    row_slot = jnp.where(live_slot, row_ids, row_count)
    col_slot = jnp.where(live_slot, col_ids, col_count)
    row_scale = jnp.ones((row_length,), jnp.float32)
    col_scale = jnp.ones((col_length,), jnp.float32)
    for pass_index in range(RUIZ_PASSES):
        row_part = pick_tiles(row_scale, row_slot, row_count)
        col_part = pick_tiles(col_scale, col_slot, col_count)
        scaled = jnp.abs(values).astype(jnp.float32) * row_part[:, :, None] * col_part[:, None, :]
        row_peak = lax.pmax(tile_peaks(jnp.max(scaled, axis=2), row_slot, row_count), "col")
        col_peak = lax.pmax(tile_peaks(jnp.max(scaled, axis=1), col_slot, col_count), "row")
        row_scale = row_scale / jnp.sqrt(row_peak + SMALL_EPS)
        col_scale = col_scale / jnp.sqrt(col_peak + SMALL_EPS)
    scaled_cost = col_scale * cost_vec
    scaled_demand = row_scale * demand
    cost_square = jnp.sum(scaled_cost * scaled_cost)
    demand_square = jnp.sum(scaled_demand * scaled_demand)
    cost_total = lax.psum(cost_square, "col")
    demand_total = lax.psum(demand_square, "row")
    norm_ratio = jnp.sqrt(cost_total + SMALL_EPS) / jnp.sqrt(demand_total + SMALL_EPS)
    primal_step = STEP_SCALE / norm_ratio
    dual_step = STEP_SCALE * norm_ratio
    primal = primal_start / col_scale
    dual_now = dual_start / row_scale
    low_side = lower / col_scale
    high_side = upper / col_scale
    for pass_index in range(ITERS):
        weights = (row_scale * dual_now).astype(jnp.bfloat16)
        picked = pick_tiles(weights, row_slot, row_count)
        partial_value = tile_sums(
            jnp.einsum("kij,ki->kj", values, picked, preferred_element_type=jnp.float32),
            col_slot,
            col_count,
        )
        gradient = col_scale * lax.psum(partial_value, "row")
        primal_next = project_bounds(
            primal - primal_step * (scaled_cost - gradient), low_side, high_side, bound_kind
        )
        shifted = (col_scale * (2.0 * primal_next - primal)).astype(jnp.bfloat16)
        picked = pick_tiles(shifted, col_slot, col_count)
        partial_value = tile_sums(
            jnp.einsum("kij,kj->ki", values, picked, preferred_element_type=jnp.float32),
            row_slot,
            row_count,
        )
        row_image = row_scale * lax.psum(partial_value, "col")
        dual_now = jnp.maximum(dual_now + dual_step * (scaled_demand - row_image), 0.0)
        primal = primal_next
    return (col_scale * primal, row_scale * dual_now)


def solution(mesh):
    return jax.shard_map(
        per_device,
        mesh=mesh,
        in_specs=(
            P("row", "col", None, None, None),
            P("row", "col", None),
            P("row", "col", None),
            P("col"),
            P("row"),
            P("col"),
            P("col"),
            P("col"),
            P("col"),
            P("row"),
        ),
        out_specs=(P("col"), P("row")),
        check_vma=False,
    )
```

profile of v0, /device:TPU:1, one launch (start us, length us, event | category | flops | bytes accessed | tf_op | source)
XLA Modules:
  0.0 670.1 jit_solution(2063073004390619092)
XLA Ops:
  8.1 0.7 gather_fusion.1
  8.8 0.7 gather_fusion
  9.6 12.0 %fusion.1 = (f32[256,128]{1,0:T(8,128)S(1)}, f32[256,128]{1,0:T(8,128)S(1)}) fusion(f32[256,128]{1,0:T(8,128)S(1)} %gather_fusion.1, f32[256,128]{1,0:T(8,128)S(1)} %gather_fusion, bf16[1,1,256,128,128]{4,3,2,1,0:T(8,128)(2,1)} %param.10), kind=kLoop, calls=%fused_computation.19 | loop fusion | flops 25100288 | bytes 8912896 | tf_op jit(solution)/shard_map/reduce_max | solution.py:80
  21.5 1.6 scatter_custom_fusion.1
  23.1 0.7 slice_bitcast_fusion.6
  23.9 1.6 scatter_custom_fusion
  25.5 0.7 slice_bitcast_fusion.7
  26.4 58.9 %all-reduce.18.cloned.1.call-done = f32[65536]{0:T(1024)} async-done(((f32[65536]{0:T(1024)}), f32[65536]{0:T(1024)}) %all-reduce.18.cloned.1.call-update) | async-done | bytes 262160 | tf_op jit(solution)/shard_map/pmax | solution.py:80
  85.2 1.1 fusion.16
  86.3 0.7 gather_fusion.2
  87.0 86.7 %all-reduce.16.cloned.1.call-done = f32[65536]{0:T(1024)} async-done(((f32[65536]{0:T(1024)}), f32[65536]{0:T(1024)}) %all-reduce.16.cloned.1.call-update) | async-done | bytes 262160 | tf_op jit(solution)/shard_map/pmax | solution.py:81
  173.7 1.0 fusion.15
  174.8 0.7 gather_fusion.3
  175.5 11.9 %fusion.4 = (f32[256,128]{1,0:T(8,128)S(1)}, f32[256,128]{1,0:T(8,128)S(1)}) fusion(f32[256,128]{1,0:T(8,128)S(1)} %gather_fusion.3, f32[256,128]{1,0:T(8,128)S(1)} %gather_fusion.2, bf16[1,1,256,128,128]{4,3,2,1,0:T(8,128)(2,1)} %param.10), kind=kLoop, calls=%fused_computation.22 | loop fusion | flops 25100288 | bytes 8912896 | tf_op jit(solution)/shard_map/reduce_max | solution.py:80
  187.4 1.6 scatter_custom_fusion.3
  189.0 0.7 slice_bitcast_fusion.4
  189.8 1.6 scatter_custom_fusion.2
  191.4 0.7 slice_bitcast_fusion.5
  192.2 56.4 %all-reduce.22.cloned.1.call-done = f32[65536]{0:T(1024)} async-done(((f32[65536]{0:T(1024)}), f32[65536]{0:T(1024)}) %all-reduce.22.cloned.1.call-update) | async-done | bytes 262160 | tf_op jit(solution)/shard_map/pmax | solution.py:80
  248.6 1.7 multiply_reduce_fusion
  250.4 0.9 gather_fusion.4
  251.2 5.6 fusion.12
  256.9 1.6 scatter_custom_fusion.4
  258.5 0.7 slice_bitcast_fusion.3
  259.3 34.0 %psum.43 = f32[]{:T(128)} all-reduce(f32[]{:T(128)} %get-tuple-element.12), channel_id=1, replica_groups=mesh['row'=16,'col'=8] {'row'}, use_global_device_ids=true, to_apply=%region_15.16 | all-reduce | flops 1 | bytes 8 | tf_op jit(solution)/shard_map/psum | solution.py:89
  294.0 43.0 %all-reduce.20.cloned.1.call-done = f32[65536]{0:T(1024)} async-done(((f32[65536]{0:T(1024)}), f32[65536]{0:T(1024)}) %all-reduce.20.cloned.1.call-update) | async-done | bytes 262160 | tf_op jit(solution)/shard_map/pmax | solution.py:81
  337.0 1.6 multiply_reduce_fusion.1
  338.6 14.5 %psum.42 = f32[]{:T(128)} all-reduce(f32[]{:T(128)} %get-tuple-element.15), channel_id=1, replica_groups=mesh['row'=16,'col'=8] {'col'}, use_global_device_ids=true, to_apply=%region_10.11 | all-reduce | flops 1 | bytes 8 | tf_op jit(solution)/shard_map/psum | solution.py:88
  353.9 70.3 %all-reduce.24.cloned.1.call-done = f32[65536]{0:T(1024)} async-done(((f32[65536]{0:T(1024)}), f32[65536]{0:T(1024)}) %all-reduce.24.cloned.1.call-update) | async-done | bytes 262160 | tf_op jit(solution)/shard_map/psum | solution.py:105
  424.2 1.2 fusion.39
  425.5 0.9 gather_fusion.5
  426.3 7.8 %fusion.10 = f32[256,1,128]{2,1,0:T(1,128)S(1)} fusion(bf16[1,1,256,128,128]{4,3,2,1,0:T(8,128)(2,1)} %param.10, bf16[256,128,1]{1,0,2:T(8,128)(2,1)S(1)} %bitcast.68), kind=kOutput, calls=%fused_computation.28 | convolution fusion | flops 8388608 | bytes 8585216 | tf_op jit(solution)/shard_map/kij,kj->ki/dot_general | solution.py:112
  434.1 1.6 scatter_custom_fusion.5
  435.7 0.7 slice_bitcast_fusion.2
  436.5 58.7 %all-reduce.26.cloned.1.call-done = f32[65536]{0:T(1024)} async-done(((f32[65536]{0:T(1024)}), f32[65536]{0:T(1024)}) %all-reduce.26.cloned.1.call-update) | async-done | bytes 262160 | tf_op jit(solution)/shard_map/psum | solution.py:116
  495.2 1.0 fusion.34
  496.2 0.9 gather_fusion.6
  497.1 5.6 fusion.8
  502.7 1.6 scatter_custom_fusion.6
  504.4 0.7 slice_bitcast_fusion.1
  505.2 84.8 %all-reduce.28.cloned.1.call-done = f32[65536]{0:T(1024)} async-done(((f32[65536]{0:T(1024)}), f32[65536]{0:T(1024)}) %all-reduce.28.cloned.1.call-update) | async-done | bytes 262160 | tf_op jit(solution)/shard_map/psum | solution.py:105
  589.9 1.9 fusion.40
  591.8 0.9 gather_fusion.7
  592.7 7.8 %fusion.6 = f32[256,1,128]{2,1,0:T(1,128)S(1)} fusion(bf16[1,1,256,128,128]{4,3,2,1,0:T(8,128)(2,1)} %param.10, bf16[256,128,1]{1,0,2:T(8,128)(2,1)S(1)} %bitcast.66), kind=kOutput, calls=%fused_computation.24 | convolution fusion | flops 8388608 | bytes 8585216 | tf_op jit(solution)/shard_map/kij,kj->ki/dot_general | solution.py:112
  600.4 1.6 scatter_custom_fusion.7
  602.1 0.7 slice_bitcast_fusion
  602.8 58.7 %all-reduce.30.cloned.1.call-done = f32[65536]{0:T(1024)} async-done(((f32[65536]{0:T(1024)}), f32[65536]{0:T(1024)}) %all-reduce.30.cloned.1.call-update) | async-done | bytes 262160 | tf_op jit(solution)/shard_map/psum | solution.py:116
  661.5 1.8 maximum_multiply_fusion
  (51 shorter events, 1.5 us)
Async XLA Ops:
  7.2 78.1 %all-reduce.18.cloned.1.call-start = ((), (), s32[]{:S(2)}) async-start(), calls=%async_computation.1 | async-start | bytes 524288 | tf_op jit(solution)/shard_map/pmax | solution.py:80
  23.9 224.7 %copy-start.4 = (f32[65536]{0:T(1024)S(1)}, f32[65536]{0:T(1024)}, u32[]{:S(2)}) copy-start(f32[65536]{0:T(1024)} %param.14) | copy-start | bytes 786436
  23.9 149.8 %all-reduce.16.cloned.1.call-start = ((), (), s32[]{:S(2)}) async-start(), calls=%async_computation | async-start | bytes 524288 | tf_op jit(solution)/shard_map/pmax | solution.py:81
  26.3 224.0 %copy-start.5 = (f32[65536]{0:T(1024)S(1)}, f32[65536]{0:T(1024)}, u32[]{:S(2)}) copy-start(f32[65536]{0:T(1024)} %param.19) | copy-start | bytes 786436
  26.3 222.3 %all-reduce.22.cloned.1.call-start = ((), (), s32[]{:S(2)}) async-start(), calls=%async_computation.3 | async-start | bytes 524288 | tf_op jit(solution)/shard_map/pmax | solution.py:80
  85.2 163.4 %copy-start.2 = (f32[65536]{0:T(1024)S(1)}, f32[65536]{0:T(1024)}, u32[]{:S(2)}) copy-start(f32[65536]{0:T(1024)} %all-reduce.18.cloned.1.call-done) | copy-start | bytes 786436
  187.4 149.6 %copy-start.1 = (f32[65536]{0:T(1024)S(1)}, f32[65536]{0:T(1024)}, u32[]{:S(2)}) copy-start(f32[65536]{0:T(1024)} %all-reduce.16.cloned.1.call-done) | copy-start | bytes 786436
  187.4 149.6 %copy-start.6 = (f32[65536]{0:T(1024)S(1)}, f32[65536]{0:T(1024)}, u32[]{:S(2)}) copy-start(f32[65536]{0:T(1024)} %param.13) | copy-start | bytes 786436
  187.4 236.8 %copy-start.7 = (f32[65536]{0:T(1024)S(1)}, f32[65536]{0:T(1024)}, u32[]{:S(2)}) copy-start(f32[65536]{0:T(1024)} %param.18) | copy-start | bytes 786436
  187.4 236.8 %copy-start.8 = (f32[65536]{0:T(1024)S(1)}, f32[65536]{0:T(1024)}, u32[]{:S(2)}) copy-start(f32[65536]{0:T(1024)} %param.15) | copy-start | bytes 786436
  187.4 236.8 %copy-start.9 = (s32[65536]{0:T(1024)S(1)}, s32[65536]{0:T(1024)}, u32[]{:S(2)}) copy-start(s32[65536]{0:T(1024)} %param.17) | copy-start | bytes 786436
  187.4 236.8 %copy-start.10 = (f32[65536]{0:T(1024)S(1)}, f32[65536]{0:T(1024)}, u32[]{:S(2)}) copy-start(f32[65536]{0:T(1024)} %param.16) | copy-start | bytes 786436
  189.8 147.2 %all-reduce.20.cloned.1.call-start = ((), (), s32[]{:S(2)}) async-start(), calls=%async_computation.2 | async-start | bytes 524288 | tf_op jit(solution)/shard_map/pmax | solution.py:81
  192.2 232.0 %all-reduce.24.cloned.1.call-start = ((), (), s32[]{:S(2)}) async-start(), calls=%async_computation.4 | async-start | bytes 524288 | tf_op jit(solution)/shard_map/psum | solution.py:105
  259.2 236.0 %all-reduce.26.cloned.1.call-start = ((), (), s32[]{:S(2)}) async-start(), calls=%async_computation.5 | async-start | bytes 524288 | tf_op jit(solution)/shard_map/psum | solution.py:116
  434.1 155.8 %copy-start = (f32[65536]{0:T(1024)S(1)}, f32[65536]{0:T(1024)}, u32[]{:S(2)}) copy-start(f32[65536]{0:T(1024)} %all-reduce.24.cloned.1.call-done) | copy-start | bytes 786436
  436.5 153.4 %all-reduce.28.cloned.1.call-start = ((), (), s32[]{:S(2)}) async-start(), calls=%async_computation.6 | async-start | bytes 524288 | tf_op jit(solution)/shard_map/psum | solution.py:105
  502.7 158.8 %copy-start.3 = (f32[65536]{0:T(1024)S(1)}, f32[65536]{0:T(1024)}, u32[]{:S(2)}) copy-start(f32[65536]{0:T(1024)} %all-reduce.26.cloned.1.call-done) | copy-start | bytes 786436
  505.1 156.4 %all-reduce.30.cloned.1.call-start = ((), (), s32[]{:S(2)}) async-start(), calls=%async_computation.7 | async-start | bytes 524288 | tf_op jit(solution)/shard_map/psum | solution.py:116
Sparse Core Ops, SparseCore 0:
  24.0 61.1 all-reduce.17
  89.3 84.3 all-reduce.15
  189.9 58.6 all-reduce.21
  252.5 84.3 all-reduce.19
  340.6 83.6 all-reduce.23
  436.6 58.5 all-reduce.25
  505.2 84.6 all-reduce.27
  602.9 58.5 all-reduce.29
where the time goes:
time: 672 us; the launch traced here: 670 us
  waiting for transfers between devices  518 us (77%)
  other arithmetic  48.7 us (7%)
  blocking collectives  48.5 us (7%)
  matrix products  26.8 us (4%)
  between operations  15.8 us (2%)
  local copies, waits for them, and re-layouts  12.4 us (2%)
    psum x2, waiting for transfers between devices, per_device(): gradient = col_scale * lax.psum(partial_value, 'row')  155 us
    pmax x2, waiting for transfers between devices, per_device(): lax.pmax(tile_peaks(jnp.max(scaled, axis=1), col_slot, col_count), 'row')  130 us
    psum x2, waiting for transfers between devices, per_device(): row_image = row_scale * lax.psum(partial_value, 'col')  117 us
    pmax x2, waiting for transfers between devices, per_device(): lax.pmax(tile_peaks(jnp.max(scaled, axis=2), row_slot, row_count), 'col')  115 us
    psum x1, blocking collectives, per_device(): demand_total = lax.psum(demand_square, 'row')  34 us
    reduce_max x2, other arithmetic, per_device(): jnp.max(scaled, axis=2)  23.8 us
    dot_general x2, matrix products, per_device(): jnp.einsum('kij,kj->ki', values, picked, preferred_element_type=jnp.float32)  15.6 us
    psum x1, blocking collectives, per_device(): cost_total = lax.psum(cost_square, 'col')  14.5 us
  transfers between devices with their start and end apart: 8, of which 8 were waited for; matrix products, arithmetic and copies ran while one was open for 3% of the time, Pallas kernels for 0%

commit v1 on v0

v1 whole, which is shorter than its diff:
```python
import functools

import jax
import jax.numpy as jnp
from jax import lax
from jax.experimental import pallas as pl
from jax.experimental.pallas import tpu as pltpu
from jax.sharding import PartitionSpec as P

SMALL_EPS = 1e-06
STEP_SCALE = 0.3
LANES = 128
GROUP = 16
CHUNKS = 8
MESH = pl.DeviceIdType.MESH
F32, BF16, I32 = jnp.float32, jnp.bfloat16, jnp.int32


def iota(shape, axis):
    return lax.broadcasted_iota(I32, shape, axis)


def dot(left, right):
    return jnp.dot(left, right, preferred_element_type=F32)


def one_hot(mask):
    return jnp.where(mask, 1.0, 0.0).astype(BF16)


def select_dot(selector, values):
    high = values.astype(BF16)
    low = (values - high.astype(F32)).astype(BF16)
    width = values.shape[1]
    both = dot(selector, jnp.concatenate([high, low], axis=1))
    return both[:, :width] + both[:, width:]


def across(column, width):
    return jnp.concatenate([column] * (width // LANES), axis=1)


def build_index(ids_ref, spread, gather, order, sorted_ids, last):
    tiles, slots = spread.shape
    lane_ids = ids_ref[...]
    column = jnp.broadcast_to(lane_ids.astype(F32), (LANES, slots)).T.astype(I32)
    spread[...] = one_hot(iota((tiles, slots), 0) == lane_ids)
    gather[...] = one_hot(iota((slots, tiles), 1) == across(column, tiles))
    wide = across(column, slots)
    down, right = iota((slots, slots), 0), iota((slots, slots), 1)
    before = (wide < lane_ids) | ((wide == lane_ids) & (down < right))
    rank = jnp.sum(jnp.where(before, 1.0, 0.0), axis=0, keepdims=True).astype(I32)
    sorter = one_hot(down == rank)
    order[...] = sorter
    coarse = (column >> 4) << 4
    parts = jnp.concatenate([coarse, column - coarse], axis=1).astype(F32).astype(BF16)
    both = dot(sorter, parts)
    in_order = both[:, :LANES] + both[:, LANES:]
    sorted_ids[...] = in_order
    following = pltpu.roll(in_order, slots - 1, 0)
    ends = (following != in_order) | (iota((slots, LANES), 0) == slots - 1)
    keys = jnp.where(ends, in_order, -5.0).T[0:1].astype(I32)
    last[...] = one_hot(iota((tiles, slots), 0) == keys)


def tile_peaks(terms, order, sorted_ids, last, exact):
    slots = terms.shape[0]
    pick = (lambda s, x: dot(s, x.astype(BF16))) if exact else select_dot
    run = pick(order[...], terms)
    ids = sorted_ids[...]
    shift = 1
    while shift < slots:
        same = pltpu.roll(ids, shift, 0) == ids
        run = jnp.maximum(run, jnp.where(same, pltpu.roll(run, shift, 0), 0.0))
        shift *= 2
    return pick(last[...], run)


def kernel(
    n_row, n_col,
    values, rows, cols, cost, demand, lower, upper, kind, primal_start, dual_start,
    primal_out, dual_out,
    kv, row_ids, col_ids, dual_full,
    cost_s, lower_s, upper_s, kind_s, primal_s, demand_s, dual_s,
    spread_r, gather_r, order_r, sorted_r, last_r,
    spread_c, gather_c, order_c, sorted_c, last_c,
    term_a, term_b, pick_a, pick_b, pick_h,
    part_r1, part_c1, part_g1, part_r2, part_c2, part_3, part_4, part_5,
    recv_r1, recv_c1, recv_g1, recv_r2, recv_c2, recv_3, recv_4, recv_5,
    full_r1, full_c1, full_2, full_3, full_4, own_primal, own_dual,
    norm_own, norm_mid, norm_x1, norm_x2,
    local_sem, chunk_sem, send_sem, recv_sem,
):
    p, q = lax.axis_index("row"), lax.axis_index("col")
    slots = kv.shape[0]
    row_tiles, col_tiles = dual_full.shape[0], part_c1.shape[0]
    row_sh, col_sh = row_tiles // n_col, col_tiles // n_row
    row_at = pl.ds(pl.multiple_of(q * row_sh, 8), row_sh)
    col_at = pl.ds(pl.multiple_of(p * col_sh, 8), col_sh)
    chunk = slots // CHUNKS

    def peer(axis, d):
        if axis == "row":
            at = lax.rem(p + d, n_row)
            return at, (at, q)
        at = lax.rem(q + d, n_col)
        return at, (p, at)

    def count(axis):
        return n_row if axis == "row" else n_col

    barrier = pltpu.get_barrier_semaphore()
    for axis in ("row", "col"):
        def greet(d, carry, axis=axis):
            pl.semaphore_signal(barrier, inc=1, device_id=peer(axis, d)[1], device_id_type=MESH)
            return carry
        lax.fori_loop(1, count(axis), greet, 0)

    local = [
        (rows, row_ids), (cols, col_ids), (dual_start, dual_full),
        (cost.at[col_at], cost_s), (lower.at[col_at], lower_s), (upper.at[col_at], upper_s),
        (kind.at[col_at], kind_s), (primal_start.at[col_at], primal_s),
        (demand.at[row_at], demand_s), (dual_start.at[row_at], dual_s),
    ]
    local = [pltpu.make_async_copy(src, dst, local_sem.at[i]) for i, (src, dst) in enumerate(local)]
    local[0].start()
    local[1].start()
    loads = []
    for i in range(CHUNKS):
        part = pl.ds(i * chunk, chunk)
        loads.append(pltpu.make_async_copy(values.at[part], kv.at[part], chunk_sem.at[i]))
        loads[-1].start()
    for copy in local[2:]:
        copy.start()

    class Exchange:
        def __init__(self, number, axis, copy):
            self.number, self.axis, self.copy = number, axis, copy

        def each(self, act):
            def body(d, carry):
                at, device = peer(self.axis, d)
                src, dst = self.copy(d, at)
                act(pltpu.make_async_remote_copy(
                    src_ref=src, dst_ref=dst, send_sem=send_sem.at[self.number, d],
                    recv_sem=recv_sem.at[self.number, d], device_id=device, device_id_type=MESH))
                return carry
            lax.fori_loop(1, count(self.axis), body, 0)

        def start(self):
            self.each(lambda c: c.start())

        def wait_recv(self):
            self.each(lambda c: c.wait_recv())

        def wait_send(self):
            self.each(lambda c: c.wait_send())

    def scatter(number, axis, part, recv):
        size = recv.shape[1]
        return Exchange(number, axis, lambda d, at: (
            part.at[pl.ds(pl.multiple_of(at * size, 8), size)], recv.at[d]))

    def spread_out(number, axis, src, dst):
        return Exchange(number, axis, lambda d, at: (src, dst))

    def collect(exchange, part, at, recv, combine):
        exchange.wait_recv()
        total = part[at, :]
        for d in range(1, recv.shape[0]):
            total = combine(total, recv[d])
        return total

    eye = iota((LANES, LANES), 0) == iota((LANES, LANES), 1)

    def on_diagonal(per_row):
        return jnp.max(jnp.where(eye, per_row, 0.0), axis=0, keepdims=True)

    def products(picked, terms, transposed):
        def body(g, carry):
            base = pl.multiple_of(g * GROUP, GROUP)
            left = picked[pl.ds(base, GROUP), :]
            place = iota((GROUP, LANES), 0)
            total = jnp.zeros((GROUP, LANES), F32)
            for b in range(GROUP):
                block = kv[base + b]
                dims = (((1,), (0,)), ((), ())) if transposed else (((1,), (1,)), ((), ()))
                result = lax.dot_general(left, block, dims, preferred_element_type=F32)
                total = jnp.where(place == b, result, total)
            terms[pl.ds(base, GROUP), :] = total
            return carry
        lax.fori_loop(0, slots // GROUP, body, 0)

    local[0].wait()
    build_index(row_ids, spread_r, gather_r, order_r, sorted_r, last_r)
    local[1].wait()
    build_index(col_ids, spread_c, gather_c, order_c, sorted_c, last_c)

    eighth = 8
    def first_peaks(g, carry):
        base = pl.multiple_of(g * eighth, eighth)
        place = iota((eighth, LANES), 0)
        by_row = jnp.zeros((eighth, LANES), F32)
        by_col = jnp.zeros((eighth, LANES), F32)
        for b in range(eighth):
            size = jnp.abs(kv[base + b].astype(F32))
            by_row = jnp.where(place == b, on_diagonal(jnp.max(size, axis=1, keepdims=True)), by_row)
            by_col = jnp.where(place == b, jnp.max(size, axis=0, keepdims=True), by_col)
        term_a[pl.ds(base, eighth), :] = by_row
        term_b[pl.ds(base, eighth), :] = by_col
        return carry
    per_chunk = chunk // eighth
    for i in range(CHUNKS):
        loads[i].wait()
        lax.fori_loop(i * per_chunk, (i + 1) * per_chunk, first_peaks, 0)

    part_r1[...] = tile_peaks(term_a[...], order_r, sorted_r, last_r, True)
    pl.semaphore_wait(barrier, n_row + n_col - 2)
    send_r1 = scatter(0, "col", part_r1, recv_r1)
    send_r1.start()
    part_c1[...] = tile_peaks(term_b[...], order_c, sorted_c, last_c, True)
    send_c1 = scatter(1, "row", part_c1, recv_c1)
    send_c1.start()

    for copy in local[2:]:
        copy.wait()
    pick_h[...] = dot(gather_r[...], dual_full[...].astype(BF16)).astype(BF16)
    products(pick_h, term_a, True)
    part_g1[...] = select_dot(spread_c[...], term_a[...])

    row_scale = 1.0 / jnp.sqrt(collect(send_r1, part_r1, row_at, recv_r1, jnp.maximum) + SMALL_EPS)
    full_r1[row_at, :] = row_scale
    share_r1 = spread_out(2, "col", full_r1.at[row_at], full_r1.at[row_at])
    share_r1.start()
    col_scale = 1.0 / jnp.sqrt(collect(send_c1, part_c1, col_at, recv_c1, jnp.maximum) + SMALL_EPS)
    full_c1[col_at, :] = col_scale
    share_c1 = spread_out(3, "row", full_c1.at[col_at], full_c1.at[col_at])
    share_c1.start()
    send_g1 = scatter(4, "row", part_g1, recv_g1)
    send_g1.start()

    share_r1.wait_recv()
    pick_a[...] = select_dot(gather_r[...], full_r1[...])
    share_c1.wait_recv()
    pick_b[...] = select_dot(gather_c[...], full_c1[...])

    def second_peaks(g, carry):
        base = pl.multiple_of(g * eighth, eighth)
        place = iota((eighth, LANES), 0)
        by_row = jnp.zeros((eighth, LANES), F32)
        by_col = jnp.zeros((eighth, LANES), F32)
        row_part = pick_a[pl.ds(base, eighth), :]
        col_part = pick_b[pl.ds(base, eighth), :]
        row_down = row_part.T
        for b in range(eighth):
            size = jnp.abs(kv[base + b].astype(F32))
            across_peak = jnp.max(size * col_part[b:b + 1], axis=1, keepdims=True)
            down_peak = jnp.max(size * row_down[:, b:b + 1], axis=0, keepdims=True)
            by_row = jnp.where(place == b, on_diagonal(across_peak), by_row)
            by_col = jnp.where(place == b, down_peak, by_col)
        term_a[pl.ds(base, eighth), :] = by_row * row_part
        term_b[pl.ds(base, eighth), :] = by_col * col_part
        return carry
    lax.fori_loop(0, slots // eighth, second_peaks, 0)

    part_r2[...] = tile_peaks(term_a[...], order_r, sorted_r, last_r, False)
    send_r2 = scatter(5, "col", part_r2, recv_r2)
    send_r2.start()
    part_c2[...] = tile_peaks(term_b[...], order_c, sorted_c, last_c, False)
    send_c2 = scatter(6, "row", part_c2, recv_c2)
    send_c2.start()
    row_scale = row_scale / jnp.sqrt(collect(send_r2, part_r2, row_at, recv_r2, jnp.maximum) + SMALL_EPS)
    col_scale = col_scale / jnp.sqrt(collect(send_c2, part_c2, col_at, recv_c2, jnp.maximum) + SMALL_EPS)

    scaled_cost = col_scale * cost_s[...]
    scaled_demand = row_scale * demand_s[...]

    def squares(x):
        return jnp.sum((x * x).reshape(-1, 8, LANES), axis=0)
    norm_own[0:8, :] = squares(scaled_cost)
    norm_own[8:16, :] = squares(scaled_demand)
    norm_1 = Exchange(7, "col", lambda d, at: (norm_own, norm_x1.at[d]))
    norm_1.start()
    primal = primal_s[...] / col_scale
    dual_now = dual_s[...] / row_scale
    low_side = lower_s[...] / col_scale
    high_side = upper_s[...] / col_scale
    bound = kind_s[...]
    norm_mid[...] = collect(norm_1, norm_own, slice(None), norm_x1, jnp.add)
    norm_2 = Exchange(8, "row", lambda d, at: (norm_mid, norm_x2.at[d]))
    norm_2.start()
    gradient = col_scale * collect(send_g1, part_g1, col_at, recv_g1, jnp.add)
    norms = collect(norm_2, norm_mid, slice(None), norm_x2, jnp.add)
    cost_total = jnp.sum(jnp.sum(norms[0:8], axis=0, keepdims=True), axis=1, keepdims=True)
    demand_total = jnp.sum(jnp.sum(norms[8:16], axis=0, keepdims=True), axis=1, keepdims=True)
    norm_ratio = jnp.sqrt(cost_total + SMALL_EPS) / jnp.sqrt(demand_total + SMALL_EPS)
    primal_step = STEP_SCALE / norm_ratio
    dual_step = STEP_SCALE * norm_ratio

    def project(x):
        x = jnp.where((bound == 1) | (bound == 3), jnp.maximum(x, low_side), x)
        return jnp.where((bound == 2) | (bound == 3), jnp.minimum(x, high_side), x)

    def forward(number, full, terms, part, recv):
        share = spread_out(number, "row", full.at[col_at], full.at[col_at])
        share.start()
        return share

    def image(share, number, full, part, recv):
        share.wait_recv()
        pick_h[...] = dot(gather_c[...], full[...].astype(BF16)).astype(BF16)
        products(pick_h, term_a, False)
        part[...] = select_dot(spread_r[...], term_a[...])
        send = scatter(number, "col", part, recv)
        send.start()
        return send

    primal_next = project(primal - primal_step * (scaled_cost - gradient))
    full_2[col_at, :] = col_scale * (2.0 * primal_next - primal)
    primal = primal_next
    share_2 = spread_out(9, "row", full_2.at[col_at], full_2.at[col_at])
    share_2.start()
    send_3 = image(share_2, 10, full_2, part_3, recv_3)
    row_image = row_scale * collect(send_3, part_3, row_at, recv_3, jnp.add)
    dual_now = jnp.maximum(dual_now + dual_step * (scaled_demand - row_image), 0.0)

    full_3[row_at, :] = row_scale * dual_now
    share_3 = spread_out(11, "col", full_3.at[row_at], full_3.at[row_at])
    share_3.start()
    share_3.wait_recv()
    pick_h[...] = dot(gather_r[...], full_3[...].astype(BF16)).astype(BF16)
    products(pick_h, term_a, True)
    part_4[...] = select_dot(spread_c[...], term_a[...])
    send_4 = scatter(12, "row", part_4, recv_4)
    send_4.start()
    gradient = col_scale * collect(send_4, part_4, col_at, recv_4, jnp.add)
    primal_next = project(primal - primal_step * (scaled_cost - gradient))
    full_4[col_at, :] = col_scale * (2.0 * primal_next - primal)
    share_4 = spread_out(13, "row", full_4.at[col_at], full_4.at[col_at])
    share_4.start()
    own_primal[...] = col_scale * primal_next
    share_p = spread_out(14, "row", own_primal, primal_out.at[col_at])
    share_p.start()
    keep_p = pltpu.make_async_copy(own_primal, primal_out.at[col_at], local_sem.at[0])
    keep_p.start()
    send_5 = image(share_4, 15, full_4, part_5, recv_5)
    row_image = row_scale * collect(send_5, part_5, row_at, recv_5, jnp.add)
    dual_now = jnp.maximum(dual_now + dual_step * (scaled_demand - row_image), 0.0)
    own_dual[...] = row_scale * dual_now
    share_d = spread_out(16, "col", own_dual, dual_out.at[row_at])
    share_d.start()
    keep_d = pltpu.make_async_copy(own_dual, dual_out.at[row_at], local_sem.at[1])
    keep_d.start()

    for exchange in (
        send_r1, send_c1, share_r1, share_c1, send_g1, send_r2, send_c2, norm_1, norm_2,
        share_2, send_3, share_3, send_4, share_4, share_p, send_5,
    ):
        exchange.wait_send()
    share_p.wait_recv()
    keep_p.wait()
    keep_d.wait()
    share_d.wait_recv()
    share_d.wait_send()


def per_device(n_row, n_col, *args):
    values, rows, cols = args[0][0, 0], args[1][0], args[2][0]
    vectors = [a.reshape(-1, LANES) for a in args[3:]]
    slots = values.shape[0]
    col_tiles, row_tiles = vectors[0].shape[0], vectors[1].shape[0]
    row_sh, col_sh = row_tiles // n_col, col_tiles // n_row
    vmem = pltpu.VMEM

    def index_scratch(tiles):
        return [
            vmem((tiles, slots), BF16), vmem((slots, tiles), BF16), vmem((slots, slots), BF16),
            vmem((slots, LANES), F32), vmem((tiles, slots), BF16),
        ]

    row_full, col_full = vmem((row_tiles, LANES), F32), vmem((col_tiles, LANES), F32)
    row_own, col_own = vmem((row_sh, LANES), F32), vmem((col_sh, LANES), F32)
    row_recv, col_recv = vmem((n_col, row_sh, LANES), F32), vmem((n_row, col_sh, LANES), F32)
    term = vmem((slots, LANES), F32)
    most = max(n_row, n_col)
    scratch = [
        vmem(values.shape, BF16), vmem((1, slots), I32), vmem((1, slots), I32), row_full,
        col_own, col_own, col_own, vmem((col_sh, LANES), I32), col_own, row_own, row_own,
        *index_scratch(row_tiles), *index_scratch(col_tiles),
        term, term, term, term, vmem((slots, LANES), BF16),
        row_full, col_full, col_full, row_full, col_full, row_full, col_full, row_full,
        row_recv, col_recv, col_recv, row_recv, col_recv, row_recv, col_recv, row_recv,
        row_full, col_full, col_full, row_full, col_full, col_own, row_own,
        vmem((16, LANES), F32), vmem((16, LANES), F32),
        vmem((n_col, 16, LANES), F32), vmem((n_row, 16, LANES), F32),
        pltpu.SemaphoreType.DMA((10,)), pltpu.SemaphoreType.DMA((CHUNKS,)),
        pltpu.SemaphoreType.DMA((17, most)), pltpu.SemaphoreType.DMA((17, most)),
    ]
    anywhere = pl.BlockSpec(memory_space=pl.ANY)
    primal, dual = pl.pallas_call(
        functools.partial(kernel, n_row, n_col),
        out_shape=(
            jax.ShapeDtypeStruct((col_tiles, LANES), F32),
            jax.ShapeDtypeStruct((row_tiles, LANES), F32),
        ),
        in_specs=[anywhere] * 10,
        out_specs=(anywhere, anywhere),
        scratch_shapes=scratch,
        compiler_params=pltpu.CompilerParams(
            collective_id=0, has_side_effects=True, vmem_limit_bytes=48 * 1024 * 1024
        ),
    )(values, rows, cols, *vectors)
    return primal.reshape(-1), dual.reshape(-1)


def solution(mesh):
    grid = P("row", "col", None)
    return jax.shard_map(
        functools.partial(per_device, mesh.shape["row"], mesh.shape["col"]),
        mesh=mesh,
        in_specs=(
            P("row", "col", None, None, None), grid, grid,
            P("col"), P("row"), P("col"), P("col"), P("col"), P("col"), P("row"),
        ),
        out_specs=(P("col"), P("row")),
        check_vma=False,
    )
```

time: 672 us -> 139 us (0.21)
  waiting for transfers between devices: 518 us -> 0 us
  Pallas kernels: 0 us -> 129 us
  other arithmetic: 48.7 us -> 0 us
  blocking collectives: 48.5 us -> 0 us
  matrix products: 26.8 us -> 0 us
  between operations: 15.8 us -> 0.66 us
    psum x4 -> x0, waiting for transfers between devices: 273 us -> none  [the longest x2 155 us: per_device(): gradient = col_scale * lax.psum(partial_value, 'row')]
    pmax x4 -> x0, waiting for transfers between devices: 245 us -> none  [the longest x2 130 us: per_device(): lax.pmax(tile_peaks(jnp.max(scaled, axis=1), col_slot, col_count), 'row')]
    pallas_call x0 -> x1, Pallas kernels: none -> 129 us  [per_device(): pl.pallas_call(functools.partial(kernel, n_row, n_col), out_shape=(jax.Sh...]
    psum x2 -> x0, blocking collectives: 48.5 us -> none  [the longest x1 34 us: per_device(): demand_total = lax.psum(demand_square, 'row')]
    dot_general x4 -> x0, matrix products: 26.8 us -> none  [the longest x2 15.6 us: per_device(): jnp.einsum('kij,kj->ki', values, picked, preferred_element_type=jnp.float32)]
    reduce_max x2 -> x0, other arithmetic: 23.8 us -> none  [per_device(): jnp.max(scaled, axis=2)]
    unnamed x22 -> x20, local copies, waits for them, and re-layouts: 0.06 us -> 9.44 us
  transfers between devices with their start and end apart: 8 -> 0, of which waited for: 8 -> 0; matrix products, arithmetic and copies ran while one was open for 3% -> 0% of each run, Pallas kernels for 0% -> 0%
where the time goes in v1:
time: 139 us
  Pallas kernels  129 us (93%)
  local copies, waits for them, and re-layouts  9.44 us (7%)
    pallas_call x1, Pallas kernels, per_device(): pl.pallas_call(functools.partial(kernel, n_row, n_col), out_shape=(jax.Sh...  129 us
    unnamed x20, local copies, waits for them, and re-layouts  9.44 us

profile of v1, /device:TPU:1, one launch (start us, length us, event | category | flops | bytes accessed | tf_op | source)
XLA Modules:
  0.0 139.0 jit_solution(4572278418959089889)
XLA Ops:
  0.6 0.0 copy-start
  0.6 0.9 copy-done
  1.6 0.0 copy-start.1
  1.6 0.9 copy-done.1
  2.5 0.0 copy-start.2
  2.5 0.9 copy-done.2
  3.5 0.0 copy-start.3
  3.5 0.9 copy-done.3
  4.4 0.0 copy-start.4
  4.4 0.9 copy-done.4
  5.4 0.0 copy-start.5
  5.4 0.9 copy-done.5
  6.3 0.0 copy-start.6
  6.3 0.9 copy-done.6
  7.3 0.0 copy-start.7
  7.3 0.7 copy-done.7
  8.0 0.0 copy-start.8
  8.0 0.7 copy-done.8
  8.6 128.9 %shard_map.113 = (f32[512,128]{1,0:T(8,128)S(1)}, f32[512,128]{1,0:T(8,128)S(1)}) custom-call(bf16[256,128,128]{2,1,0:T(8,128)(2,1)} %bitcast.23, s32[1,256]{1,0:T(1,128)S(1)} %bitcast.21, s32[1,256]{1,0:T(1,128)S(1)} %bitcast.22, f32[512,128]{1,0:T(8,128)S(1)} %bitcast.12, f32[512,128]{1,0:T(8,128)S(1)} %bitcast.13, f32[512,128]{1,0:T(8,128)S(1)} %bitcast.14, ...), custom_call_target="tpu_custom_call" | custom-call | tf_op jit(solution)/shard_map/pallas_call | solution.py:400
  137.5 0.7 copy.14
  138.3 0.7 copy.15
Async XLA Ops:
  0.6 1.0 copy-start
  1.6 0.9 copy-start.1
  2.5 0.9 copy-start.2
  3.5 0.9 copy-start.3
  4.4 0.9 copy-start.4
  5.4 0.9 copy-start.5
  6.3 0.9 copy-start.6
  7.3 0.7 copy-start.7
  8.0 0.7 copy-start.8

commit v2 on v1

--- a/solution.py
+++ b/solution.py
@@ -80,14 +80,14 @@
     n_row, n_col,
     values, rows, cols, cost, demand, lower, upper, kind, primal_start, dual_start,
     primal_out, dual_out,
-    kv, row_ids, col_ids, dual_full,
-    cost_s, lower_s, upper_s, kind_s, primal_s, demand_s, dual_s,
+    kv, kvt, row_ids, col_ids, dual_full,
+    cost_f, lower_f, upper_f, kind_f, primal_f, slope_f, demand_s, dual_s,
     spread_r, gather_r, order_r, sorted_r, last_r,
     spread_c, gather_c, order_c, sorted_c, last_c,
     term_a, term_b, pick_a, pick_b, pick_h,
     part_r1, part_c1, part_g1, part_r2, part_c2, part_3, part_4, part_5,
     recv_r1, recv_c1, recv_g1, recv_r2, recv_c2, recv_3, recv_4, recv_5,
-    full_r1, full_c1, full_2, full_3, full_4, own_primal, own_dual,
+    full_r1, full_c1, full_c2, full_g1, full_2, full_3, full_4, own_primal, own_dual,
     norm_own, norm_mid, norm_x1, norm_x2,
     local_sem, chunk_sem, send_sem, recv_sem,
 ):
@@ -99,12 +99,22 @@
     col_at = pl.ds(pl.multiple_of(p * col_sh, 8), col_sh)
     chunk = slots // CHUNKS
 
+    def ring(axis):
+        count = n_row if axis == "row" else n_col
+        return (count // 4, 4) if axis == "row" and count >= 16 else (count // 2, 2)
+
     def peer(axis, d):
-        if axis == "row":
-            at = lax.rem(p + d, n_row)
-            return at, (at, q)
-        at = lax.rem(q + d, n_col)
-        return at, (p, at)
+        first, second = ring(axis)
+        own = p if axis == "row" else q
+        at = lax.rem(own // second + d // second, first) * second + lax.rem(own % second + d % second, second)
+        return at, ((at, q) if axis == "row" else (p, at))
+
+    def farthest_first(axis):
+        first, second = ring(axis)
+        def hops(d):
+            one, two = d // second, d % second
+            return min(one, first - one) + (min(two, second - two) if axis == "row" else 0)
+        return sorted(range(1, first * second), key=hops, reverse=True)
 
     def count(axis):
         return n_row if axis == "row" else n_col
@@ -118,8 +128,7 @@
 
     local = [
         (rows, row_ids), (cols, col_ids), (dual_start, dual_full),
-        (cost.at[col_at], cost_s), (lower.at[col_at], lower_s), (upper.at[col_at], upper_s),
-        (kind.at[col_at], kind_s), (primal_start.at[col_at], primal_s),
+        (cost, cost_f), (lower, lower_f), (upper, upper_f), (kind, kind_f), (primal_start, primal_f),
         (demand.at[row_at], demand_s), (dual_start.at[row_at], dual_s),
     ]
     local = [pltpu.make_async_copy(src, dst, local_sem.at[i]) for i, (src, dst) in enumerate(local)]
@@ -137,7 +146,7 @@
         def __init__(self, number, axis, copy):
             self.number, self.axis, self.copy = number, axis, copy
 
-        def each(self, act):
+        def each(self, act, unrolled=True):
             def body(d, carry):
                 at, device = peer(self.axis, d)
                 src, dst = self.copy(d, at)
@@ -145,7 +154,11 @@
                     src_ref=src, dst_ref=dst, send_sem=send_sem.at[self.number, d],
                     recv_sem=recv_sem.at[self.number, d], device_id=device, device_id_type=MESH))
                 return carry
-            lax.fori_loop(1, count(self.axis), body, 0)
+            if unrolled:
+                for d in farthest_first(self.axis):
+                    body(d, 0)
+            else:
+                lax.fori_loop(1, count(self.axis), body, 0)
 
         def start(self):
             self.each(lambda c: c.start())
@@ -154,7 +167,7 @@
             self.each(lambda c: c.wait_recv())
 
         def wait_send(self):
-            self.each(lambda c: c.wait_send())
+            self.each(lambda c: c.wait_send(), False)
 
     def scatter(number, axis, part, recv):
         size = recv.shape[1]
@@ -171,25 +184,32 @@
             total = combine(total, recv[d])
         return total
 
+    def down_max(block):
+        folded = jnp.max(block.reshape(-1, 16, LANES), axis=0)
+        return jnp.max(folded.astype(F32), axis=0, keepdims=True)
+
     eye = iota((LANES, LANES), 0) == iota((LANES, LANES), 1)
 
     def on_diagonal(per_row):
         return jnp.max(jnp.where(eye, per_row, 0.0), axis=0, keepdims=True)
 
-    def products(picked, terms, transposed):
+    def products(picked, terms, blocks):
         def body(g, carry):
             base = pl.multiple_of(g * GROUP, GROUP)
             left = picked[pl.ds(base, GROUP), :]
             place = iota((GROUP, LANES), 0)
+            even = place % 2 == 0
+            left = left.astype(F32)
+            left = jnp.concatenate([jnp.where(even, left, 0.0), jnp.where(even, 0.0, left)], axis=1).astype(BF16)
             total = jnp.zeros((GROUP, LANES), F32)
-            for b in range(GROUP):
-                block = kv[base + b]
-                dims = (((1,), (0,)), ((), ())) if transposed else (((1,), (1,)), ((), ()))
-                result = lax.dot_general(left, block, dims, preferred_element_type=F32)
-                total = jnp.where(place == b, result, total)
+            for b in range(0, GROUP, 4):
+                pair = [blocks[pl.ds(base + b + i, 2)].reshape(2 * LANES, LANES) for i in (0, 2)]
+                result = dot(left, jnp.concatenate(pair, axis=1))
+                total = jnp.where(place // 2 == b // 2, result[:, :LANES], total)
+                total = jnp.where(place // 2 == b // 2 + 1, result[:, LANES:], total)
             terms[pl.ds(base, GROUP), :] = total
             return carry
-        lax.fori_loop(0, slots // GROUP, body, 0)
+        lax.fori_loop(0, slots // GROUP, body, 0, unroll=slots // GROUP)
 
     local[0].wait()
     build_index(row_ids, spread_r, gather_r, order_r, sorted_r, last_r)
@@ -203,9 +223,11 @@
         by_row = jnp.zeros((eighth, LANES), F32)
         by_col = jnp.zeros((eighth, LANES), F32)
         for b in range(eighth):
-            size = jnp.abs(kv[base + b].astype(F32))
-            by_row = jnp.where(place == b, on_diagonal(jnp.max(size, axis=1, keepdims=True)), by_row)
-            by_col = jnp.where(place == b, jnp.max(size, axis=0, keepdims=True), by_col)
+            block = kv[base + b]
+            turned = block.T
+            kvt[base + b] = turned
+            by_row = jnp.where(place == b, down_max(jnp.abs(turned)), by_row)
+            by_col = jnp.where(place == b, down_max(jnp.abs(block)), by_col)
         term_a[pl.ds(base, eighth), :] = by_row
         term_b[pl.ds(base, eighth), :] = by_col
         return carry
@@ -214,18 +236,18 @@
         loads[i].wait()
         lax.fori_loop(i * per_chunk, (i + 1) * per_chunk, first_peaks, 0)
 
+    part_c1[...] = tile_peaks(term_b[...], order_c, sorted_c, last_c, True)
+    pl.semaphore_wait(barrier, n_row + n_col - 2)
+    send_c1 = scatter(1, "row", part_c1, recv_c1)
+    send_c1.start()
     part_r1[...] = tile_peaks(term_a[...], order_r, sorted_r, last_r, True)
-    pl.semaphore_wait(barrier, n_row + n_col - 2)
     send_r1 = scatter(0, "col", part_r1, recv_r1)
     send_r1.start()
-    part_c1[...] = tile_peaks(term_b[...], order_c, sorted_c, last_c, True)
-    send_c1 = scatter(1, "row", part_c1, recv_c1)
-    send_c1.start()
 
     for copy in local[2:]:
         copy.wait()
     pick_h[...] = dot(gather_r[...], dual_full[...].astype(BF16)).astype(BF16)
-    products(pick_h, term_a, True)
+    products(pick_h, term_a, kv)
     part_g1[...] = select_dot(spread_c[...], term_a[...])
 
     row_scale = 1.0 / jnp.sqrt(collect(send_r1, part_r1, row_at, recv_r1, jnp.maximum) + SMALL_EPS)
@@ -244,6 +266,9 @@
     share_c1.wait_recv()
     pick_b[...] = select_dot(gather_c[...], full_c1[...])
 
+    wide_at = (2 * eighth, eighth * LANES)
+    spreader = one_hot(iota(wide_at, 0) % eighth == iota(wide_at, 1) // LANES)
+
     def second_peaks(g, carry):
         base = pl.multiple_of(g * eighth, eighth)
         place = iota((eighth, LANES), 0)
@@ -251,28 +276,41 @@
         by_col = jnp.zeros((eighth, LANES), F32)
         row_part = pick_a[pl.ds(base, eighth), :]
         col_part = pick_b[pl.ds(base, eighth), :]
-        row_down = row_part.T
+        high = row_part.astype(BF16).astype(F32)
+        row_down = jnp.concatenate([high, row_part - high], axis=0).T.astype(BF16)
         for b in range(eighth):
-            size = jnp.abs(kv[base + b].astype(F32))
-            across_peak = jnp.max(size * col_part[b:b + 1], axis=1, keepdims=True)
-            down_peak = jnp.max(size * row_down[:, b:b + 1], axis=0, keepdims=True)
-            by_row = jnp.where(place == b, on_diagonal(across_peak), by_row)
+            size = jnp.abs(kv[base + b].astype(F32)) * col_part[b:b + 1]
+            across_peak = on_diagonal(jnp.max(size, axis=1, keepdims=True))
+            if b % 2 == 0:
+                wide = dot(row_down, spreader[:, b * LANES:(b + 2) * LANES])
+            size = jnp.abs(kv[base + b].astype(F32)) * wide[:, (b % 2) * LANES:(b % 2 + 1) * LANES]
+            down_peak = jnp.max(size, axis=0, keepdims=True)
+            by_row = jnp.where(place == b, across_peak, by_row)
             by_col = jnp.where(place == b, down_peak, by_col)
         term_a[pl.ds(base, eighth), :] = by_row * row_part
         term_b[pl.ds(base, eighth), :] = by_col * col_part
         return carry
-    lax.fori_loop(0, slots // eighth, second_peaks, 0)
-
+    half = slots // eighth // 2
+    lax.fori_loop(0, half, second_peaks, 0, unroll=2)
+    full_g1[col_at, :] = collect(send_g1, part_g1, col_at, recv_g1, jnp.add)
+    share_g1 = spread_out(9, "row", full_g1.at[col_at], full_g1.at[col_at])
+    share_g1.start()
+    lax.fori_loop(half, 2 * half, second_peaks, 0, unroll=2)
+
+    part_c2[...] = tile_peaks(term_b[...], order_c, sorted_c, last_c, False)
+    send_c2 = scatter(6, "row", part_c2, recv_c2)
+    send_c2.start()
     part_r2[...] = tile_peaks(term_a[...], order_r, sorted_r, last_r, False)
     send_r2 = scatter(5, "col", part_r2, recv_r2)
     send_r2.start()
-    part_c2[...] = tile_peaks(term_b[...], order_c, sorted_c, last_c, False)
-    send_c2 = scatter(6, "row", part_c2, recv_c2)
-    send_c2.start()
     row_scale = row_scale / jnp.sqrt(collect(send_r2, part_r2, row_at, recv_r2, jnp.maximum) + SMALL_EPS)
     col_scale = col_scale / jnp.sqrt(collect(send_c2, part_c2, col_at, recv_c2, jnp.maximum) + SMALL_EPS)
 
-    scaled_cost = col_scale * cost_s[...]
+    full_c2[col_at, :] = col_scale
+    share_c2 = spread_out(17, "row", full_c2.at[col_at], full_c2.at[col_at])
+    share_c2.start()
+
+    scaled_cost = col_scale * cost_f[col_at, :]
     scaled_demand = row_scale * demand_s[...]
 
     def squares(x):
@@ -281,15 +319,21 @@
     norm_own[8:16, :] = squares(scaled_demand)
     norm_1 = Exchange(7, "col", lambda d, at: (norm_own, norm_x1.at[d]))
     norm_1.start()
-    primal = primal_s[...] / col_scale
     dual_now = dual_s[...] / row_scale
-    low_side = lower_s[...] / col_scale
-    high_side = upper_s[...] / col_scale
-    bound = kind_s[...]
     norm_mid[...] = collect(norm_1, norm_own, slice(None), norm_x1, jnp.add)
     norm_2 = Exchange(8, "row", lambda d, at: (norm_mid, norm_x2.at[d]))
     norm_2.start()
-    gradient = col_scale * collect(send_g1, part_g1, col_at, recv_g1, jnp.add)
+
+    share_g1.wait_recv()
+    share_c2.wait_recv()
+    step_rows = 64
+    for i in range(0, col_tiles, step_rows):
+        at = pl.ds(i, step_rows)
+        scale = full_c2[at, :]
+        primal_f[at, :] = primal_f[at, :] / scale
+        lower_f[at, :] = lower_f[at, :] / scale
+        upper_f[at, :] = upper_f[at, :] / scale
+        slope_f[at, :] = scale * cost_f[at, :] - scale * full_g1[at, :]
     norms = collect(norm_2, norm_mid, slice(None), norm_x2, jnp.add)
     cost_total = jnp.sum(jnp.sum(norms[0:8], axis=0, keepdims=True), axis=1, keepdims=True)
     demand_total = jnp.sum(jnp.sum(norms[8:16], axis=0, keepdims=True), axis=1, keepdims=True)
@@ -297,30 +341,28 @@
     primal_step = STEP_SCALE / norm_ratio
     dual_step = STEP_SCALE * norm_ratio
 
-    def project(x):
-        x = jnp.where((bound == 1) | (bound == 3), jnp.maximum(x, low_side), x)
-        return jnp.where((bound == 2) | (bound == 3), jnp.minimum(x, high_side), x)
-
-    def forward(number, full, terms, part, recv):
-        share = spread_out(number, "row", full.at[col_at], full.at[col_at])
-        share.start()
-        return share
-
-    def image(share, number, full, part, recv):
-        share.wait_recv()
-        pick_h[...] = dot(gather_c[...], full[...].astype(BF16)).astype(BF16)
-        products(pick_h, term_a, False)
+    def project(x, at):
+        bound = kind_f[at, :]
+        x = jnp.where((bound == 1) | (bound == 3), jnp.maximum(x, lower_f[at, :]), x)
+        return jnp.where((bound == 2) | (bound == 3), jnp.minimum(x, upper_f[at, :]), x)
+
+    for i in range(0, col_tiles, step_rows):
+        at = pl.ds(i, step_rows)
+        primal = primal_f[at, :]
+        primal_next = project(primal - primal_step * slope_f[at, :], at)
+        full_2[at, :] = (full_c2[at, :] * (2.0 * primal_next - primal)).astype(BF16)
+        primal_f[at, :] = primal_next
+
+    def image(number, shifted, part, recv):
+        pick_h[...] = dot(gather_c[...], shifted).astype(BF16)
+        products(pick_h, term_a, kvt)
         part[...] = select_dot(spread_r[...], term_a[...])
         send = scatter(number, "col", part, recv)
         send.start()
         return send
 
-    primal_next = project(primal - primal_step * (scaled_cost - gradient))
-    full_2[col_at, :] = col_scale * (2.0 * primal_next - primal)
-    primal = primal_next
-    share_2 = spread_out(9, "row", full_2.at[col_at], full_2.at[col_at])
-    share_2.start()
-    send_3 = image(share_2, 10, full_2, part_3, recv_3)
+    send_3 = image(10, full_2[...], part_3, recv_3)
+    primal = primal_f[col_at, :]
     row_image = row_scale * collect(send_3, part_3, row_at, recv_3, jnp.add)
     dual_now = jnp.maximum(dual_now + dual_step * (scaled_demand - row_image), 0.0)
 
@@ -329,12 +371,12 @@
     share_3.start()
     share_3.wait_recv()
     pick_h[...] = dot(gather_r[...], full_3[...].astype(BF16)).astype(BF16)
-    products(pick_h, term_a, True)
+    products(pick_h, term_a, kv)
     part_4[...] = select_dot(spread_c[...], term_a[...])
     send_4 = scatter(12, "row", part_4, recv_4)
     send_4.start()
     gradient = col_scale * collect(send_4, part_4, col_at, recv_4, jnp.add)
-    primal_next = project(primal - primal_step * (scaled_cost - gradient))
+    primal_next = project(primal - primal_step * (scaled_cost - gradient), col_at)
     full_4[col_at, :] = col_scale * (2.0 * primal_next - primal)
     share_4 = spread_out(13, "row", full_4.at[col_at], full_4.at[col_at])
     share_4.start()
@@ -343,7 +385,8 @@
     share_p.start()
     keep_p = pltpu.make_async_copy(own_primal, primal_out.at[col_at], local_sem.at[0])
     keep_p.start()
-    send_5 = image(share_4, 15, full_4, part_5, recv_5)
+    share_4.wait_recv()
+    send_5 = image(15, full_4[...].astype(BF16), part_5, recv_5)
     row_image = row_scale * collect(send_5, part_5, row_at, recv_5, jnp.add)
     dual_now = jnp.maximum(dual_now + dual_step * (scaled_demand - row_image), 0.0)
     own_dual[...] = row_scale * dual_now
@@ -354,7 +397,7 @@
 
     for exchange in (
         send_r1, send_c1, share_r1, share_c1, send_g1, send_r2, send_c2, norm_1, norm_2,
-        share_2, send_3, share_3, send_4, share_4, share_p, send_5,
+        share_g1, share_c2, send_3, share_3, send_4, share_4, share_p, send_5,
     ):
         exchange.wait_send()
     share_p.wait_recv()
@@ -384,19 +427,19 @@
     term = vmem((slots, LANES), F32)
     most = max(n_row, n_col)
     scratch = [
-        vmem(values.shape, BF16), vmem((1, slots), I32), vmem((1, slots), I32), row_full,
-        col_own, col_own, col_own, vmem((col_sh, LANES), I32), col_own, row_own, row_own,
+        vmem(values.shape, BF16), vmem(values.shape, BF16), vmem((1, slots), I32), vmem((1, slots), I32), row_full,
+        col_full, col_full, col_full, vmem((col_tiles, LANES), I32), col_full, col_full, row_own, row_own,
         *index_scratch(row_tiles), *index_scratch(col_tiles),
         term, term, term, term, vmem((slots, LANES), BF16),
         row_full, col_full, col_full, row_full, col_full, row_full, col_full, row_full,
         row_recv, col_recv, col_recv, row_recv, col_recv, row_recv, col_recv, row_recv,
-        row_full, col_full, col_full, row_full, col_full, col_own, row_own,
+        row_full, col_full, col_full, col_full, vmem((col_tiles, LANES), BF16), row_full, col_full, col_own, row_own,
         vmem((16, LANES), F32), vmem((16, LANES), F32),
         vmem((n_col, 16, LANES), F32), vmem((n_row, 16, LANES), F32),
         pltpu.SemaphoreType.DMA((10,)), pltpu.SemaphoreType.DMA((CHUNKS,)),
-        pltpu.SemaphoreType.DMA((17, most)), pltpu.SemaphoreType.DMA((17, most)),
+        pltpu.SemaphoreType.DMA((18, most)), pltpu.SemaphoreType.DMA((18, most)),
     ]
-    anywhere = pl.BlockSpec(memory_space=pl.ANY)
+    anywhere = pl.BlockSpec(memory_space=pltpu.HBM)
     primal, dual = pl.pallas_call(
         functools.partial(kernel, n_row, n_col),
         out_shape=(
@@ -407,7 +450,7 @@
         out_specs=(anywhere, anywhere),
         scratch_shapes=scratch,
         compiler_params=pltpu.CompilerParams(
-            collective_id=0, has_side_effects=True, vmem_limit_bytes=48 * 1024 * 1024
+            collective_id=0, has_side_effects=True, vmem_limit_bytes=60 * 1024 * 1024
         ),
     )(values, rows, cols, *vectors)
     return primal.reshape(-1), dual.reshape(-1)

time: 139 us -> 95.4 us (0.69)
  Pallas kernels: 129 us -> 91.2 us
  local copies, waits for them, and re-layouts: 9.44 us -> 3.34 us
    pallas_call x1, Pallas kernels: 129 us -> 91.2 us  [per_device(): pl.pallas_call(functools.partial(kernel, n_row, n_col), out_shape=(jax.Sh...]
    unnamed x20 -> x2, local copies, waits for them, and re-layouts: 9.44 us -> 3.34 us
where the time goes in v2:
time: 95.4 us; the launch traced here: 95.2 us
  Pallas kernels  91.2 us (96%)
  local copies, waits for them, and re-layouts  3.34 us (4%)
    pallas_call x1, Pallas kernels, per_device(): pl.pallas_call(functools.partial(kernel, n_row, n_col), out_shape=(jax.Sh...  91.2 us
    unnamed x2, local copies, waits for them, and re-layouts  3.34 us

profile of v2, /device:TPU:1, one launch (start us, length us, event | category | flops | bytes accessed | tf_op | source)
XLA Modules:
  0.0 95.2 jit_solution(6540192718165171728)
XLA Ops:
  0.6 91.2 %shard_map.113 = (f32[512,128]{1,0:T(8,128)}, f32[512,128]{1,0:T(8,128)}) custom-call(bf16[256,128,128]{2,1,0:T(8,128)(2,1)} %bitcast.12, s32[1,256]{1,0:T(1,128)} %bitcast.22, s32[1,256]{1,0:T(1,128)} %bitcast.23, f32[512,128]{1,0:T(8,128)} %bitcast.13, f32[512,128]{1,0:T(8,128)} %bitcast.14, f32[512,128]{1,0:T(8,128)} %bitcast.15, f32[512,128]{1,0:T(8,128)} %bitcast.16, ...), custom_call_target="tpu_custom_call" | custom-call | tf_op jit(solution)/shard_map/pallas_call | solution.py:443
  91.9 1.7 %copy.14 = f32[65536]{0:T(1024)} copy(f32[65536]{0:T(1024)} %bitcast.21) | data formatting | bytes 524288
  93.6 1.7 %copy.15 = f32[65536]{0:T(1024)} copy(f32[65536]{0:T(1024)} %bitcast.20) | data formatting | bytes 524288

commit v3 on v2

--- a/solution.py
+++ b/solution.py
@@ -169,10 +169,12 @@
         def wait_send(self):
             self.each(lambda c: c.wait_send(), False)
 
-    def scatter(number, axis, part, recv):
+    def scatter(number, axis, part, recv, piece=0, pieces=1):
         size = recv.shape[1]
+        step = size // pieces
         return Exchange(number, axis, lambda d, at: (
-            part.at[pl.ds(pl.multiple_of(at * size, 8), size)], recv.at[d]))
+            part.at[pl.ds(pl.multiple_of(at * size + piece * step, 8), step)],
+            recv.at[d, pl.ds(piece * step, step)]))
 
     def spread_out(number, axis, src, dst):
         return Exchange(number, axis, lambda d, at: (src, dst))
@@ -191,7 +193,10 @@
     eye = iota((LANES, LANES), 0) == iota((LANES, LANES), 1)
 
     def on_diagonal(per_row):
-        return jnp.max(jnp.where(eye, per_row, 0.0), axis=0, keepdims=True)
+        chosen = jnp.zeros((8, LANES), F32)
+        for i in range(0, LANES, 8):
+            chosen = jnp.where(eye[i:i + 8], per_row[i:i + 8], chosen)
+        return jnp.max(chosen, axis=0, keepdims=True)
 
     def products(picked, terms, blocks):
         def body(g, carry):
@@ -277,10 +282,18 @@
         row_part = pick_a[pl.ds(base, eighth), :]
         col_part = pick_b[pl.ds(base, eighth), :]
         high = row_part.astype(BF16).astype(F32)
+        high2 = col_part.astype(BF16).astype(F32)
+        col_down = jnp.concatenate([high2, col_part - high2], axis=0).T.astype(BF16)
         row_down = jnp.concatenate([high, row_part - high], axis=0).T.astype(BF16)
         for b in range(eighth):
-            size = jnp.abs(kv[base + b].astype(F32)) * col_part[b:b + 1]
-            across_peak = on_diagonal(jnp.max(size, axis=1, keepdims=True))
+            if b % 4 < 2:
+                if b % 2 == 0:
+                    wide2 = dot(col_down, spreader[:, b * LANES:(b + 2) * LANES])
+                size = jnp.abs(kvt[base + b].astype(F32)) * wide2[:, (b % 2) * LANES:(b % 2 + 1) * LANES]
+                across_peak = jnp.max(size, axis=0, keepdims=True)
+            else:
+                size = jnp.abs(kv[base + b].astype(F32)) * col_part[b:b + 1]
+                across_peak = on_diagonal(jnp.max(size, axis=1, keepdims=True))
             if b % 2 == 0:
                 wide = dot(row_down, spreader[:, b * LANES:(b + 2) * LANES])
             size = jnp.abs(kv[base + b].astype(F32)) * wide[:, (b % 2) * LANES:(b % 2 + 1) * LANES]
@@ -291,11 +304,11 @@
         term_b[pl.ds(base, eighth), :] = by_col * col_part
         return carry
     half = slots // eighth // 2
-    lax.fori_loop(0, half, second_peaks, 0, unroll=2)
+    lax.fori_loop(0, half, second_peaks, 0, unroll=4)
     full_g1[col_at, :] = collect(send_g1, part_g1, col_at, recv_g1, jnp.add)
     share_g1 = spread_out(9, "row", full_g1.at[col_at], full_g1.at[col_at])
     share_g1.start()
-    lax.fori_loop(half, 2 * half, second_peaks, 0, unroll=2)
+    lax.fori_loop(half, 2 * half, second_peaks, 0, unroll=4)
 
     part_c2[...] = tile_peaks(term_b[...], order_c, sorted_c, last_c, False)
     send_c2 = scatter(6, "row", part_c2, recv_c2)
@@ -353,23 +366,44 @@
         full_2[at, :] = (full_c2[at, :] * (2.0 * primal_next - primal)).astype(BF16)
         primal_f[at, :] = primal_next
 
-    def image(number, shifted, part, recv):
+    half_sh = row_sh // 2
+    halves = [slice(h * half_sh, (h + 1) * half_sh) for h in range(2)]
+    half_at = [pl.ds(pl.multiple_of(q * row_sh + h * half_sh, 8), half_sh) for h in range(2)]
+
+    def image(numbers, shifted, part, recv):
         pick_h[...] = dot(gather_c[...], shifted).astype(BF16)
         products(pick_h, term_a, kvt)
-        part[...] = select_dot(spread_r[...], term_a[...])
-        send = scatter(number, "col", part, recv)
-        send.start()
-        return send
-
-    send_3 = image(10, full_2[...], part_3, recv_3)
+        sends = []
+        for h in range(2):
+            starts = range(h * half_sh, row_tiles, row_sh)
+            selector = jnp.concatenate([spread_r[i:i + half_sh, :] for i in starts], axis=0)
+            sums = select_dot(selector, term_a[...])
+            for j, i in enumerate(starts):
+                part[i:i + half_sh, :] = sums[j * half_sh:(j + 1) * half_sh]
+            sends.append(scatter(numbers[h], "col", part, recv, h, 2))
+            sends[h].start()
+        return sends
+
+    def next_dual(h, send, part, recv, dual):
+        send.wait_recv()
+        total = part[half_at[h], :]
+        for d in range(1, n_col):
+            total = total + recv[d, halves[h], :]
+        own = halves[h]
+        return jnp.maximum(dual[own] + dual_step * (scaled_demand[own] - row_scale[own] * total), 0.0)
+
+    send_3 = image((10, 18), full_2[...], part_3, recv_3)
     primal = primal_f[col_at, :]
-    row_image = row_scale * collect(send_3, part_3, row_at, recv_3, jnp.add)
-    dual_now = jnp.maximum(dual_now + dual_step * (scaled_demand - row_image), 0.0)
-
-    full_3[row_at, :] = row_scale * dual_now
-    share_3 = spread_out(11, "col", full_3.at[row_at], full_3.at[row_at])
-    share_3.start()
-    share_3.wait_recv()
+
+    duals, share_3 = [], []
+    for h in range(2):
+        duals.append(next_dual(h, send_3[h], part_3, recv_3, dual_now))
+        full_3[half_at[h], :] = row_scale[halves[h]] * duals[h]
+        share_3.append(spread_out((11, 19)[h], "col", full_3.at[half_at[h]], full_3.at[half_at[h]]))
+        share_3[h].start()
+    dual_now = jnp.concatenate(duals, axis=0)
+    for share in share_3:
+        share.wait_recv()
     pick_h[...] = dot(gather_r[...], full_3[...].astype(BF16)).astype(BF16)
     products(pick_h, term_a, kv)
     part_4[...] = select_dot(spread_c[...], term_a[...])
@@ -386,25 +420,46 @@
     keep_p = pltpu.make_async_copy(own_primal, primal_out.at[col_at], local_sem.at[0])
     keep_p.start()
     share_4.wait_recv()
-    send_5 = image(15, full_4[...].astype(BF16), part_5, recv_5)
-    row_image = row_scale * collect(send_5, part_5, row_at, recv_5, jnp.add)
-    dual_now = jnp.maximum(dual_now + dual_step * (scaled_demand - row_image), 0.0)
-    own_dual[...] = row_scale * dual_now
-    share_d = spread_out(16, "col", own_dual, dual_out.at[row_at])
-    share_d.start()
-    keep_d = pltpu.make_async_copy(own_dual, dual_out.at[row_at], local_sem.at[1])
-    keep_d.start()
+    send_5 = image((15, 20), full_4[...].astype(BF16), part_5, recv_5)
+    share_d, keep_d = [], []
+    for h in range(2):
+        own_dual[halves[h], :] = row_scale[halves[h]] * next_dual(h, send_5[h], part_5, recv_5, dual_now)
+        source, target = own_dual.at[pl.ds(h * half_sh, half_sh)], dual_out.at[half_at[h]]
+        share_d.append(spread_out((16, 21)[h], "col", source, target))
+        share_d[h].start()
+        keep_d.append(pltpu.make_async_copy(source, target, local_sem.at[1 + h]))
+        keep_d[h].start()
 
     for exchange in (
-        send_r1, send_c1, share_r1, share_c1, send_g1, send_r2, send_c2, norm_1, norm_2,
-        share_g1, share_c2, send_3, share_3, send_4, share_4, share_p, send_5,
+        send_r1, send_c1, share_r1, share_c1, send_g1, share_g1, send_r2, send_c2, share_c2, norm_1, norm_2,
+        *send_3, *share_3, send_4, share_4, share_p, *send_5,
     ):
         exchange.wait_send()
     share_p.wait_recv()
     keep_p.wait()
-    keep_d.wait()
-    share_d.wait_recv()
-    share_d.wait_send()
+    for h in range(2):
+        keep_d[h].wait()
+    for share in share_d:
+        share.wait_recv()
+    for share in share_d:
+        share.wait_send()
+
+
+def keep(primal, dual, primal_out, dual_out, primal_held, dual_held, sems):
+    reads, writes = [], []
+    for source, held, target in ((primal, primal_held, primal_out), (dual, dual_held, dual_out)):
+        half = held.shape[0] // 2
+        for start in (0, half):
+            at, number = pl.ds(start, half), len(reads)
+            reads.append(pltpu.make_async_copy(source.at[at], held.at[at], sems.at[number]))
+            writes.append(pltpu.make_async_copy(held.at[at], target.at[at], sems.at[4 + number]))
+    for read in reads:
+        read.start()
+    for read, write in zip(reads, writes):
+        read.wait()
+        write.start()
+    for write in writes:
+        write.wait()
 
 
 def per_device(n_row, n_col, *args):
@@ -437,7 +492,7 @@
         vmem((16, LANES), F32), vmem((16, LANES), F32),
         vmem((n_col, 16, LANES), F32), vmem((n_row, 16, LANES), F32),
         pltpu.SemaphoreType.DMA((10,)), pltpu.SemaphoreType.DMA((CHUNKS,)),
-        pltpu.SemaphoreType.DMA((18, most)), pltpu.SemaphoreType.DMA((18, most)),
+        pltpu.SemaphoreType.DMA((22, most)), pltpu.SemaphoreType.DMA((22, most)),
     ]
     anywhere = pl.BlockSpec(memory_space=pltpu.HBM)
     primal, dual = pl.pallas_call(
@@ -453,6 +508,16 @@
             collective_id=0, has_side_effects=True, vmem_limit_bytes=60 * 1024 * 1024
         ),
     )(values, rows, cols, *vectors)
+    primal, dual = pl.pallas_call(
+        keep,
+        out_shape=(
+            jax.ShapeDtypeStruct((col_tiles, LANES), F32),
+            jax.ShapeDtypeStruct((row_tiles, LANES), F32),
+        ),
+        in_specs=[anywhere] * 2,
+        out_specs=(anywhere, anywhere),
+        scratch_shapes=[col_full, row_full, pltpu.SemaphoreType.DMA((8,))],
+    )(primal, dual)
     return primal.reshape(-1), dual.reshape(-1)
 
 

time: 95.4 us -> 91.9 us (0.963)
  local copies, waits for them, and re-layouts: 3.34 us -> 0 us
    unnamed x2 -> x0, local copies, waits for them, and re-layouts: 3.34 us -> none
    pallas_call x1, Pallas kernels: 91.2 us -> 89.2 us  [per_device(): pl.pallas_call(functools.partial(kernel, n_row, n_col), out_shape=(jax.Sh...]
    pallas_call x0 -> x1, Pallas kernels: none -> 1.82 us  [per_device(): pl.pallas_call(keep, out_shape=(jax.ShapeDtypeStruct((col_tiles, LANES),...]
where the time goes in v3:
time: 91.9 us; the launch traced here: 91.8 us
  Pallas kernels  91 us (99%)
    pallas_call x1, Pallas kernels, per_device(): pl.pallas_call(functools.partial(kernel, n_row, n_col), out_shape=(jax.Sh...  89.2 us

profile of v3, /device:TPU:1, one launch (start us, length us, event | category | flops | bytes accessed | tf_op | source)
XLA Modules:
  0.0 91.8 jit_solution(9641480697127920593)
XLA Ops:
  0.6 89.2 %shard_map.113 = (f32[512,128]{1,0:T(8,128)}, f32[512,128]{1,0:T(8,128)}) custom-call(bf16[256,128,128]{2,1,0:T(8,128)(2,1)} %bitcast.12, s32[1,256]{1,0:T(1,128)} %bitcast.20, s32[1,256]{1,0:T(1,128)} %bitcast.21, f32[512,128]{1,0:T(8,128)} %bitcast.13, f32[512,128]{1,0:T(8,128)} %bitcast.14, f32[512,128]{1,0:T(8,128)} %bitcast.15, f32[512,128]{1,0:T(8,128)} %bitcast.16, ...), custom_call_target="tpu_custom_call" | custom-call | tf_op jit(solution)/shard_map/pallas_call | solution.py:498
  89.8 1.8 %shard_map.114 = (f32[512,128]{1,0:T(8,128)}, f32[512,128]{1,0:T(8,128)}) custom-call(f32[512,128]{1,0:T(8,128)} %get-tuple-element.6.primal, f32[512,128]{1,0:T(8,128)} %get-tuple-element.7.dual), custom_call_target="tpu_custom_call" | custom-call | tf_op jit(solution)/shard_map/pallas_call | solution.py:511

commit v4 on v3

--- a/solution.py
+++ b/solution.py
@@ -121,10 +121,8 @@
 
     barrier = pltpu.get_barrier_semaphore()
     for axis in ("row", "col"):
-        def greet(d, carry, axis=axis):
+        for d in farthest_first(axis):
             pl.semaphore_signal(barrier, inc=1, device_id=peer(axis, d)[1], device_id_type=MESH)
-            return carry
-        lax.fori_loop(1, count(axis), greet, 0)
 
     local = [
         (rows, row_ids), (cols, col_ids), (dual_start, dual_full),
@@ -263,12 +261,12 @@
     full_c1[col_at, :] = col_scale
     share_c1 = spread_out(3, "row", full_c1.at[col_at], full_c1.at[col_at])
     share_c1.start()
-    send_g1 = scatter(4, "row", part_g1, recv_g1)
-    send_g1.start()
 
     share_r1.wait_recv()
     pick_a[...] = select_dot(gather_r[...], full_r1[...])
     share_c1.wait_recv()
+    send_g1 = scatter(4, "row", part_g1, recv_g1)
+    send_g1.start()
     pick_b[...] = select_dot(gather_c[...], full_c1[...])
 
     wide_at = (2 * eighth, eighth * LANES)
@@ -303,12 +301,12 @@
         term_a[pl.ds(base, eighth), :] = by_row * row_part
         term_b[pl.ds(base, eighth), :] = by_col * col_part
         return carry
-    half = slots // eighth // 2
-    lax.fori_loop(0, half, second_peaks, 0, unroll=4)
+    most = slots // eighth // 4 * 3
+    lax.fori_loop(0, most, second_peaks, 0, unroll=4)
     full_g1[col_at, :] = collect(send_g1, part_g1, col_at, recv_g1, jnp.add)
     share_g1 = spread_out(9, "row", full_g1.at[col_at], full_g1.at[col_at])
     share_g1.start()
-    lax.fori_loop(half, 2 * half, second_peaks, 0, unroll=4)
+    lax.fori_loop(most, slots // eighth, second_peaks, 0, unroll=4)
 
     part_c2[...] = tile_peaks(term_b[...], order_c, sorted_c, last_c, False)
     send_c2 = scatter(6, "row", part_c2, recv_c2)
@@ -415,12 +413,12 @@
     share_4 = spread_out(13, "row", full_4.at[col_at], full_4.at[col_at])
     share_4.start()
     own_primal[...] = col_scale * primal_next
-    share_p = spread_out(14, "row", own_primal, primal_out.at[col_at])
-    share_p.start()
     keep_p = pltpu.make_async_copy(own_primal, primal_out.at[col_at], local_sem.at[0])
     keep_p.start()
     share_4.wait_recv()
     send_5 = image((15, 20), full_4[...].astype(BF16), part_5, recv_5)
+    share_p = spread_out(14, "row", own_primal, primal_out.at[col_at])
+    share_p.start()
     share_d, keep_d = [], []
     for h in range(2):
         own_dual[halves[h], :] = row_scale[halves[h]] * next_dual(h, send_5[h], part_5, recv_5, dual_now)

time: 91.9 us -> 90.5 us (0.985)
  Pallas kernels: 91 us -> 89.7 us
    pallas_call x1, Pallas kernels: 89.2 us -> 87.9 us  [per_device(): pl.pallas_call(functools.partial(kernel, n_row, n_col), out_shape=(jax.Sh...]
where the time goes in v4:
time: 90.5 us; the launch traced here: 90.3 us
  Pallas kernels  89.7 us (99%)
    pallas_call x1, Pallas kernels, per_device(): pl.pallas_call(functools.partial(kernel, n_row, n_col), out_shape=(jax.Sh...  87.9 us
    pallas_call x1, Pallas kernels, per_device(): pl.pallas_call(keep, out_shape=(jax.ShapeDtypeStruct((col_tiles, LANES),...  1.82 us

profile of v4, /device:TPU:1, one launch (start us, length us, event | category | flops | bytes accessed | tf_op | source)
XLA Modules:
  0.0 90.3 jit_solution(16598887306561512818)
XLA Ops:
  0.6 87.9 %shard_map.113 = (f32[512,128]{1,0:T(8,128)}, f32[512,128]{1,0:T(8,128)}) custom-call(bf16[256,128,128]{2,1,0:T(8,128)(2,1)} %bitcast.12, s32[1,256]{1,0:T(1,128)} %bitcast.20, s32[1,256]{1,0:T(1,128)} %bitcast.21, f32[512,128]{1,0:T(8,128)} %bitcast.13, f32[512,128]{1,0:T(8,128)} %bitcast.14, f32[512,128]{1,0:T(8,128)} %bitcast.15, f32[512,128]{1,0:T(8,128)} %bitcast.16, ...), custom_call_target="tpu_custom_call" | custom-call | tf_op jit(solution)/shard_map/pallas_call | solution.py:496
  88.5 1.8 %shard_map.114 = (f32[512,128]{1,0:T(8,128)}, f32[512,128]{1,0:T(8,128)}) custom-call(f32[512,128]{1,0:T(8,128)} %get-tuple-element.6.primal, f32[512,128]{1,0:T(8,128)} %get-tuple-element.7.dual), custom_call_target="tpu_custom_call" | custom-call | tf_op jit(solution)/shard_map/pallas_call | solution.py:509

commit v5 on v4

--- a/solution.py
+++ b/solution.py
@@ -319,7 +319,6 @@
 
     full_c2[col_at, :] = col_scale
     share_c2 = spread_out(17, "row", full_c2.at[col_at], full_c2.at[col_at])
-    share_c2.start()
 
     scaled_cost = col_scale * cost_f[col_at, :]
     scaled_demand = row_scale * demand_s[...]
@@ -330,6 +329,7 @@
     norm_own[8:16, :] = squares(scaled_demand)
     norm_1 = Exchange(7, "col", lambda d, at: (norm_own, norm_x1.at[d]))
     norm_1.start()
+    share_c2.start()
     dual_now = dual_s[...] / row_scale
     norm_mid[...] = collect(norm_1, norm_own, slice(None), norm_x1, jnp.add)
     norm_2 = Exchange(8, "row", lambda d, at: (norm_mid, norm_x2.at[d]))

time: 90.5 us -> 90.4 us (level)
  no operation moved by 1% of the time
where the time goes in v5:
time: 90.4 us; the launch traced here: 90.2 us
  Pallas kernels  89.6 us (99%)
    pallas_call x1, Pallas kernels, per_device(): pl.pallas_call(functools.partial(kernel, n_row, n_col), out_shape=(jax.Sh...  87.8 us
    pallas_call x1, Pallas kernels, per_device(): pl.pallas_call(keep, out_shape=(jax.ShapeDtypeStruct((col_tiles, LANES),...  1.82 us

profile of v5, /device:TPU:1, one launch (start us, length us, event | category | flops | bytes accessed | tf_op | source)
XLA Modules:
  0.0 90.2 jit_solution(5496754499054590500)
XLA Ops:
  0.6 87.8 %shard_map.113 = (f32[512,128]{1,0:T(8,128)}, f32[512,128]{1,0:T(8,128)}) custom-call(bf16[256,128,128]{2,1,0:T(8,128)(2,1)} %bitcast.12, s32[1,256]{1,0:T(1,128)} %bitcast.20, s32[1,256]{1,0:T(1,128)} %bitcast.21, f32[512,128]{1,0:T(8,128)} %bitcast.13, f32[512,128]{1,0:T(8,128)} %bitcast.14, f32[512,128]{1,0:T(8,128)} %bitcast.15, f32[512,128]{1,0:T(8,128)} %bitcast.16, ...), custom_call_target="tpu_custom_call" | custom-call | tf_op jit(solution)/shard_map/pallas_call | solution.py:496
  88.4 1.8 %shard_map.114 = (f32[512,128]{1,0:T(8,128)}, f32[512,128]{1,0:T(8,128)}) custom-call(f32[512,128]{1,0:T(8,128)} %get-tuple-element.6.primal, f32[512,128]{1,0:T(8,128)} %get-tuple-element.7.dual), custom_call_target="tpu_custom_call" | custom-call | tf_op jit(solution)/shard_map/pallas_call | solution.py:509
